TPU v7x, 128 devices: a whole 4x4x4 slice. The times are simulated.
128 devices in a mesh: tok: 4 (over y), seq: 16 (over z, x), kv: 2 (over core).
Axes of the slice: x: 4, y: 4, z: 4, core: 2. Of those that a mesh axis runs over, the one named last changes fastest.
Arguments:
- token_ids: int32 [64, 4], replicated, may hold values from 0 to 32767
- request_order: int32 [64], replicated, may hold values from 0 to 63, each once
- cache_lengths: int32 [64], replicated, may hold values from 1 to 16384, 524288 in all
- embed_table: bfloat16 [32768, 2048], P(('tok', 'kv'), 'seq'), may hold values from -3 to 3
- attn_gain: bfloat16 [2048], replicated, may hold values from 0.099609375 to 1.8984375
- proj_query: bfloat16 [2048, 2048], P(None, ('tok', 'kv')), may hold values from -0.125 to 0.125
- proj_kv: bfloat16 [2048, 8, 128], P(None, ('tok', 'kv')), may hold values from -0.125 to 0.125
- kv_cache: bfloat16 [64, 16384, 8, 128], P(None, 'seq', ('tok', 'kv')), may hold values from -125 to 125, as said below
- proj_out: bfloat16 [2048, 2048], P(('tok', 'kv'), 'seq'), may hold values from -0.25 to 0.25
- mlp_gain: bfloat16 [2048], replicated, may hold values from 0.099609375 to 1.8984375
- proj_gate: bfloat16 [2048, 8192], P(None, 'seq'), may hold values from -0.125 to 0.125
- proj_up: bfloat16 [2048, 8192], P(None, 'seq'), may hold values from -0.125 to 0.125
- proj_down: bfloat16 [8192, 2048], P('seq'), may hold values from -0.0625 to 0.0625
Outputs:
- hidden_out: bfloat16 [64, 4, 2048], P(('tok', 'kv'), None, 'seq')
Inputs may be any that keep to these rules, and one draw needn't show every extreme that they name: `request_order`: every request stands in exactly one slot. `cache_lengths`: the lengths sum to 524288 and the largest equals 16384. `kv_cache`: cached keys are already rotated to their positions.
All inputs are finite; a program needn't handle non-finite values.
Results may differ from a plain program's by a relative error of at most 0.018.
The roundings to bfloat16 on the way count: a program that leaves them out, or rounds other values in their place, can miss the bound.
Values may be sent and summed in bfloat16 or wider, within the bound.
A program may use at most 128 MiB of HBM per device.

v0:
```python
import jax
import jax.numpy as jnp
from jax import lax
from jax.sharding import PartitionSpec as P

EPSILON = 1e-05
ROPE_BASE = 1000000.0
FLOOR_SCORE = -1e30


def combined_all(value, axis, join):
    pieces = jax.tree.map(lambda part: lax.all_gather(part, axis), value)
    head = jax.tree.map(lambda part: part[0], pieces)
    tail = jax.tree.map(lambda part: part[1:], pieces)
    so_far, _ = lax.scan(lambda so_far, share: (join(so_far, share), None), head, tail)
    return so_far


def rotate(vector, position):
    half_dim = vector.shape[-1] // 2
    frequency = ROPE_BASE ** (-(jnp.arange(half_dim, dtype=jnp.float32) * 2.0 / vector.shape[-1]))
    angles = position[..., None] * frequency
    cosine = jnp.cos(angles)
    sine_part = jnp.sin(angles)
    front_half = vector[..., :half_dim]
    back_half = vector[..., half_dim:]
    return jnp.concatenate(
        [front_half * cosine - back_half * sine_part, back_half * cosine + front_half * sine_part],
        axis=-1,
    )


def combine(earlier, later):
    peak_a, mass_a, accum_a = earlier
    peak_b, mass_b, accum_b = later
    highest = jnp.maximum(peak_a, peak_b)
    factor_a = jnp.exp(peak_a - highest)
    factor_b = jnp.exp(peak_b - highest)
    return (
        highest,
        mass_a * factor_a + mass_b * factor_b,
        accum_a * factor_a[..., None] + accum_b * factor_b[..., None],
    )


def per_device(
    token_ids,
    request_order,
    cache_lengths,
    embed_table,
    attn_gain,
    proj_query,
    proj_kv,
    kv_cache,
    proj_out,
    mlp_gain,
    proj_gate,
    proj_up,
    proj_down,
):
    n_req, n_steps = token_ids.shape
    width = proj_query.shape[0]
    head_dim = kv_cache.shape[-1] // 2
    group_heads = proj_query.shape[1] // head_dim
    ctx_dev = kv_cache.shape[1]
    columns = embed_table.shape[1]
    vocab_rows = embed_table.shape[0]
    scale = head_dim ** (-0.5)
    owners = lax.axis_size("tok") * lax.axis_size("kv")
    owner_index = lax.axis_index("tok") * lax.axis_size("kv") + lax.axis_index("kv")
    seq_rank = lax.axis_index("seq")
    offset = token_ids.reshape(-1) - owner_index * vocab_rows
    inside = (offset >= 0) & (offset < vocab_rows)
    picked = jnp.take(embed_table, jnp.clip(offset, 0, vocab_rows - 1), axis=0)
    partial_x = jnp.where(inside[:, None], picked.astype(jnp.float32), 0.0)
    local_x = lax.psum(partial_x.astype(jnp.bfloat16), ("tok", "kv"))
    kv_flat = proj_kv.reshape(width, -1)
    full_x = lax.all_gather(local_x, "seq", axis=1, tiled=True)
    widened = full_x.astype(jnp.float32)
    square_mean = jnp.mean(widened * widened, axis=1)
    scaled = (widened * attn_gain.astype(jnp.float32)).astype(jnp.bfloat16)
    q_raw = jnp.dot(scaled, proj_query, preferred_element_type=jnp.float32)
    kv_raw = jnp.dot(scaled, kv_flat, preferred_element_type=jnp.float32)
    inv_norm = lax.rsqrt(square_mean + EPSILON)[:, None]
    q_scaled = (q_raw * inv_norm).reshape(n_req, n_steps, group_heads, head_dim)
    kv_scaled = (kv_raw * inv_norm).reshape(n_req, n_steps, 2 * head_dim)
    position = (cache_lengths[:, None] + jnp.arange(n_steps, dtype=jnp.int32)[None, :]).astype(
        jnp.float32
    )
    query = rotate(q_scaled, position[:, :, None]).astype(jnp.bfloat16)
    new_keys = rotate(kv_scaled[..., :head_dim], position).astype(jnp.bfloat16)
    new_values = kv_scaled[..., head_dim:].astype(jnp.bfloat16)
    cache_rows = kv_cache[:, :, 0, :]
    key_part = cache_rows[..., :head_dim]
    value_part = cache_rows[..., head_dim:]
    scores = (
        jnp.einsum("rjgd,rpd->rjgp", query, key_part, preferred_element_type=jnp.float32) * scale
    )
    places = seq_rank * ctx_dev + jnp.arange(ctx_dev, dtype=jnp.int32)
    is_live = (places[None, :] < cache_lengths[:, None])[:, None, None, :]
    masked = jnp.where(is_live, scores, FLOOR_SCORE)
    block_peak = jnp.max(masked, axis=-1)
    block_weight = jnp.where(is_live, jnp.exp(masked - block_peak[..., None]), 0.0).astype(
        jnp.bfloat16
    )
    block_mass = jnp.sum(block_weight.astype(jnp.float32), axis=-1)
    block_accum = jnp.einsum(
        "rjgp,rpd->rjgd", block_weight, value_part, preferred_element_type=jnp.float32
    )
    peak_all, mass_all, accum_all = combined_all(
        (block_peak, block_mass, block_accum), "seq", combine
    )
    fresh_scores = (
        jnp.einsum("rjgd,rkd->rjgk", query, new_keys, preferred_element_type=jnp.float32) * scale
    )
    causal = (jnp.arange(n_steps)[:, None] >= jnp.arange(n_steps)[None, :])[None, :, None, :]
    fresh_masked = jnp.where(causal, fresh_scores, FLOOR_SCORE)
    fresh_peak = jnp.max(fresh_masked, axis=-1)
    fresh_weight = jnp.where(causal, jnp.exp(fresh_masked - fresh_peak[..., None]), 0.0).astype(
        jnp.bfloat16
    )
    fresh_mass = jnp.sum(fresh_weight.astype(jnp.float32), axis=-1)
    fresh_accum = jnp.einsum(
        "rjgk,rkd->rjgd", fresh_weight, new_values, preferred_element_type=jnp.float32
    )
    highest = jnp.maximum(peak_all, fresh_peak)
    cache_factor = jnp.exp(peak_all - highest)
    fresh_factor = jnp.exp(fresh_peak - highest)
    numer = accum_all * cache_factor[..., None] + fresh_accum * fresh_factor[..., None]
    denom = mass_all * cache_factor + fresh_mass * fresh_factor
    attended = (
        (numer / denom[..., None])
        .astype(jnp.bfloat16)
        .reshape(n_req, n_steps, group_heads * head_dim)
    )
    slot_rows = attended[request_order].reshape(n_req * n_steps, group_heads * head_dim)
    per_owner = n_req // owners
    attn_part = lax.psum_scatter(
        jnp.dot(slot_rows, proj_out, preferred_element_type=jnp.float32),
        ("tok", "kv"),
        scatter_dimension=0,
        tiled=True,
    )
    my_requests = lax.dynamic_slice_in_dim(request_order, owner_index * per_owner, per_owner)
    own_x = local_x.reshape(n_req, n_steps, columns)[my_requests].reshape(
        per_owner * n_steps, columns
    )
    mid = (own_x.astype(jnp.float32) + attn_part).astype(jnp.bfloat16)
    piece_wide = lax.all_gather(mid, "seq", axis=1, tiled=True).astype(jnp.float32)
    gain_part = mlp_gain.astype(jnp.float32)
    piece_scaled = (piece_wide * gain_part).astype(jnp.bfloat16)
    gate_acc = jnp.dot(piece_scaled, proj_gate, preferred_element_type=jnp.float32)
    up_acc = jnp.dot(piece_scaled, proj_up, preferred_element_type=jnp.float32)
    square_total = jnp.sum(piece_wide * piece_wide, axis=1)
    inv_mlp = lax.rsqrt(square_total / width + EPSILON)[:, None]
    hidden = (jax.nn.silu(gate_acc * inv_mlp) * (up_acc * inv_mlp)).astype(jnp.bfloat16)
    down_terms = jnp.dot(hidden, proj_down, preferred_element_type=jnp.float32)
    mlp_part = lax.psum_scatter(down_terms, "seq", scatter_dimension=1, tiled=True)
    result = (mid.astype(jnp.float32) + mlp_part).astype(jnp.bfloat16)
    return result.reshape(per_owner, n_steps, columns)


def solution(mesh):
    placed = (
        P(),
        P(),
        P(),
        P(("tok", "kv"), "seq"),
        P(),
        P(None, ("tok", "kv")),
        P(None, ("tok", "kv"), None),
        P(None, "seq", ("tok", "kv"), None),
        P(("tok", "kv"), "seq"),
        P(),
        P(None, "seq"),
        P(None, "seq"),
        P("seq", None),
    )
    return jax.shard_map(
        per_device,
        mesh=mesh,
        in_specs=placed,
        out_specs=P(("tok", "kv"), None, "seq"),
        check_vma=False,
    )
```

profile of v0, /device:TPU:0, one launch (start us, length us, event | category | flops | bytes accessed | tf_op | source)
XLA Modules:
  0.0 429.6 jit_solution(7146980658867892863)
XLA Ops:
  6.5 0.8 compare_and_fusion.1
  8.7 2.1 gather_fusion
  10.7 0.8 select_convert_fusion.1
  11.6 61.3 %all-reduce.2.cloned.1.call-done = bf16[256,128]{1,0:T(8,128)(2,1)} async-done(((bf16[256,128]{1,0:T(8,128)(2,1)}), bf16[256,128]{1,0:T(8,128)(2,1)}) %all-reduce.2.cloned.1.call-update) | async-done | bytes 65552 | tf_op jit(solution)/shard_map/psum | solution.py:76
  73.6 22.1 %copy.87 = bf16[64,1024,1,128]{1,3,0,2:T(8,128)(2,1)} copy(bf16[64,1024,1,128]{3,1,2,0:T(8,128)(2,1)} %param.22) | data formatting | bytes 33554432 | tf_op args[7]
  96.5 21.2 %all-gather.6.cloned.1.call-done = bf16[256,2048]{1,0:T(8,128)(2,1)} async-done(((bf16[256,128]{1,0:T(8,128)(2,1)}), bf16[256,2048]{1,0:T(8,128)(2,1)}) %all-gather.6.cloned.1.call-update) | async-done | bytes 1048592 | tf_op jit(solution)/shard_map/all_gather | solution.py:78
  117.7 1.5 fusion.7
  119.2 2.0 convolution_multiply_fusion.1
  121.4 1.8 convolution_multiply_fusion.2
  123.5 1.0 multiply_cosine_fusion
  125.2 6.2 %fusion.5 = (f32[64,4,4]{2,1,0:T(4,128)S(1)}, f32[64,4,4,1024]{3,2,1,0:T(4,128)S(1)}) fusion(pred[64,1024]{1,0:T(8,128)(4,1)} %broadcast_compare_fusion, bf16[64,1024,128]{1,2,0:T(8,128)(2,1)} %bitcast.67, bf16[64,4,4,32]{3,2,1,0:T(4,128)(2,1)S(1)} %get-tuple-element.101, bf16[64,4,4,32]{3,2,1,0:T(4,128)(2,1)S(1)} %get-tuple-element.100), kind=kOutput, calls=%fused_computation.18 | convolution fusion | flops 137624576 | bytes 12783616 | tf_op jit(solution)/shard_map/rjgd,rpd->rjgp/dot_general | solution.py:97
  131.4 3.7 convert_reduce_fusion
  135.1 6.8 %fusion.3 = f32[64,4,4,64]{3,2,1,0:T(4,128)} fusion(bf16[64,4,4,1024]{3,2,1,0:T(4,128)(2,1)S(1)} %get-tuple-element.99, bf16[64,1024,128]{1,2,0:T(8,128)(2,1)} %bitcast.68), kind=kOutput, calls=%fused_computation.12 | convolution fusion | flops 134217728 | bytes 10747904 | tf_op jit(solution)/shard_map/rjgp,rpd->rjgd/dot_general | solution.py:107
  142.7 30.8 %all-gather.1 = f32[1024,4,4]{2,1,0:T(4,128)S(1)} all-gather(f32[64,4,4]{2,1,0:T(4,128)S(1)} %get-tuple-element.98), channel_id=3, replica_groups=mesh['tok'=4,'seq'=16,'kv'=2] {'seq'}, dimensions={0}, use_global_device_ids=true | all-gather | bytes 69632 | tf_op jit(solution)/shard_map/all_gather | solution.py:12
  173.5 1.4 slice.76
  174.9 32.0 %all-gather = f32[1024,4,4]{2,1,0:T(4,128)S(1)} all-gather(f32[64,4,4]{2,1,0:T(4,128)S(1)} %get-tuple-element.110), channel_id=2, replica_groups=mesh['tok'=4,'seq'=16,'kv'=2] {'seq'}, dimensions={0}, use_global_device_ids=true | all-gather | bytes 69632 | tf_op jit(solution)/shard_map/all_gather | solution.py:12
  206.9 1.4 slice.75
  208.3 0.7 copy.110
  209.1 3.3 fusion.36
  212.8 0.7 convert_reduce_fusion.1
  213.6 1.0 copy.102
  214.6 2.7 copy.93
  217.4 2.2 copy.92
  219.6 5.8 %all-gather.8.cloned.1.call-done = f32[1024,4,4,64]{3,2,1,0:T(4,128)} async-done(((f32[64,4,4,64]{3,2,1,0:T(4,128)}), f32[1024,4,4,64]{3,2,1,0:T(4,128)}) %all-gather.8.cloned.1.call-update) | async-done | bytes 4194320 | tf_op jit(solution)/shard_map/all_gather | solution.py:12
  225.3 7.7 %slice.77 = f32[960,4,4,64]{3,2,1,0:T(4,128)} slice(f32[1024,4,4,64]{3,2,1,0:T(4,128)} %all-gather.8.cloned.1.call-done), slice={[64:1024], [0:4], [0:4], [0:64]} | slice | bytes 7864320 | tf_op jit(solution)/shard_map/slice | solution.py:14
  233.1 53.9 %while.14 = (s32[]{:T(128)}, f32[64,4,4]{0,2,1:T(4,128)S(1)}, f32[64,4,4]{0,2,1:T(4,128)S(1)}, f32[64,4,4,64]{3,2,1,0:T(4,128)S(1)}, f32[15,64,4,4]{1,3,2,0:T(4,...) while((s32[]{:T(128)}, f32[64,4,4]{0,2,1:T(4,128)S(1)}, ...), condition=%wide.region_5.6_spmd, body=%wide.region_4.5_spmd.sunk | while | flops 202754 | bytes 843877 | solution.py:15
  233.1 0.8 fusion.53
  234.1 2.6 fusion.54
  236.7 0.7 fusion.53
  237.7 2.6 fusion.54
  240.3 0.7 fusion.53
  241.3 2.6 fusion.54
  243.9 0.7 fusion.53
  244.9 2.6 fusion.54
  247.5 0.7 fusion.53
  248.5 2.6 fusion.54
  251.1 0.7 fusion.53
  252.1 2.6 fusion.54
  254.7 0.7 fusion.53
  255.7 2.6 fusion.54
  259.2 2.6 fusion.54
  261.8 0.7 fusion.53
  262.8 2.6 fusion.54
  265.4 0.7 fusion.53
  266.4 2.6 fusion.54
  270.0 2.6 fusion.54
  273.6 2.6 fusion.54
  276.2 0.7 fusion.53
  277.2 2.6 fusion.54
  279.8 0.7 fusion.53
  280.8 2.6 fusion.54
  284.4 2.6 fusion.54
  287.1 0.8 copy.104
  287.9 0.8 copy.107
  288.7 2.0 fusion.10
  290.9 0.8 gather_fusion.2
  291.8 0.8 fusion.41
  292.8 1.4 gather_fusion.1
  294.2 28.3 %reduce-scatter.3.cloned.1.call-done = f32[32,128]{1,0:T(8,128)} async-done(((f32[256,128]{1,0:T(8,128)}), f32[32,128]{1,0:T(8,128)}) %reduce-scatter.3.cloned.1.call-update) | async-done | bytes 16400 | tf_op jit(solution)/shard_map/reduce_scatter | solution.py:138
  323.3 23.9 %all_gather.31 = bf16[32,2048]{1,0:T(8,128)(2,1)S(1)} all-gather(bf16[32,128]{1,0:T(8,128)(2,1)S(1)} %fusion.32), channel_id=1, replica_groups=mesh['tok'=4,'seq'=16,'kv'=2] {'seq'}, dimensions={1}, use_global_device_ids=true | all-gather | bytes 139264 | tf_op jit(solution)/shard_map/all_gather | solution.py:149
  347.3 2.0 convolution_multiply_fusion.4
  349.4 3.2 fusion.13
  352.6 69.2 %reduce-scatter.5.cloned.1.call-done = f32[32,128]{1,0:T(8,128)} async-done(((f32[32,2048]{1,0:T(8,128)}), f32[32,128]{1,0:T(8,128)}) %reduce-scatter.5.cloned.1.call-update) | async-done | bytes 16400 | tf_op jit(solution)/shard_map/reduce_scatter | solution.py:158
  421.8 1.3 add_convert_fusion.2
  (110 shorter events, 13.7 us)
Async XLA Ops:
  6.5 342.8 %copy-start = (bf16[512,2048]{1,0:T(8,128)(2,1)S(1)}, bf16[512,2048]{1,0:T(8,128)(2,1)}, u32[]{:S(2)}) copy-start(bf16[512,2048]{1,0:T(8,128)(2,1)} %param.27) | copy-start | bytes 6291460
  6.5 66.3 %all-reduce.2.cloned.1.call-start = ((), (), s32[]{:S(2)}) async-start(), calls=%async_computation.2 | async-start | bytes 131072 | tf_op jit(solution)/shard_map/psum | solution.py:76
  11.5 106.1 %all-gather.6.cloned.1.call-start = ((), (), s32[]{:S(2)}) async-start(), calls=%async_computation.3 | async-start | bytes 1114112 | tf_op jit(solution)/shard_map/all_gather | solution.py:78
  72.9 152.4 %all-gather.8.cloned.1.call-start = ((), (), s32[]{:S(2)}) async-start(), calls=%async_computation.6 | async-start | bytes 8912896 | tf_op jit(solution)/shard_map/all_gather | solution.py:12
  73.6 22.1 %copy-start.7 = (s32[64]{0:T(128)S(1)}, s32[64]{0:T(128)}, u32[]{:S(2)}) copy-start(s32[64]{0:T(128)} %param.17) | copy-start | bytes 772
  125.2 6.2 %copy-start.1 = (pred[64,1024]{1,0:T(8,128)(4,1)S(1)}, pred[64,1024]{1,0:T(8,128)(4,1)}, u32[]{:S(2)}) copy-start(pred[64,1024]{1,0:T(8,128)(4,1)} %broadcast_compare_fusion) | copy-start | bytes 196612
  135.1 6.9 %copy-start.9 = (s32[64]{0:T(128)S(1)}, s32[64]{0:T(128)}, u32[]{:S(2)}) copy-start(s32[64]{0:T(128)} %param.16) | copy-start | bytes 772
  142.0 180.5 %reduce-scatter.3.cloned.1.call-start = ((), (), s32[]{:S(2)}) async-start(), calls=%async_computation.4 | async-start | bytes 147456 | tf_op jit(solution)/shard_map/reduce_scatter | solution.py:138
  142.1 70.6 %copy-start.8 = (pred[4,4]{1,0:T(4,128)(4,1)}, pred[4,4]{1,0:T(4,128)(4,1)S(1)}, u32[]{:S(2)}) copy-start(pred[4,4]{1,0:T(4,128)(4,1)S(1)} %iota_compare_fusion) | copy-start | bytes 52
  174.9 33.4 %copy-start.3 = (bf16[64,4,32]{0,2,1:T(8,128)(2,1)S(1)}, bf16[64,4,32]{0,2,1:T(8,128)(2,1)}, u32[]{:S(2)}) copy-start(bf16[64,4,32]{0,2,1:T(8,128)(2,1)} %get-tuple-element.108) | copy-start | bytes 49156
  174.9 33.4 %copy-start.4 = (bf16[64,4,32]{0,2,1:T(8,128)(2,1)S(1)}, bf16[64,4,32]{0,2,1:T(8,128)(2,1)}, u32[]{:S(2)}) copy-start(bf16[64,4,32]{0,2,1:T(8,128)(2,1)} %get-tuple-element.109) | copy-start | bytes 49156
  225.3 7.7 %slice-start = ((f32[1024,4,4,64]{3,2,1,0:T(4,128)}), f32[64,4,4,64]{3,2,1,0:T(4,128)S(1)}, s32[]{:S(2)}) async-start(f32[1024,4,4,64]{3,2,1,0:T(4,128)} %all-gather.8.cloned.1.call-done), calls=%async_computation.7 | async-start | bytes 1048576 | tf_op jit(solution)/shard_map/slice | solution.py:13
  233.1 55.7 %copy-start.2 = (bf16[64,4,4,4]{3,2,1,0:T(4,128)(2,1)S(1)}, bf16[64,4,4,4]{3,2,1,0:T(4,128)(2,1)}, u32[]{:S(2)}) copy-start(bf16[64,4,4,4]{3,2,1,0:T(4,128)(2,1)} %copy.102) | copy-start | bytes 24580
  288.7 3.1 copy-start.5
  288.7 4.0 copy-start.6
  288.7 4.0 copy-start.10
  292.6 129.1 %reduce-scatter.5.cloned.1.call-start = ((), (), s32[]{:S(2)}) async-start(), calls=%async_computation.5 | async-start | bytes 278528 | tf_op jit(solution)/shard_map/reduce_scatter | solution.py:158
Sparse Core Ops, SparseCore 0:
  11.7 61.1 all-reduce.1
  75.2 42.4 all-gather.5
  142.1 83.1 all-gather.7
  292.8 29.7 reduce-scatter.2
  352.7 68.9 reduce-scatter.4
where the time goes:
time: 432 us; the launch traced here: 430 us
  waiting for transfers between devices  186 us (43%)
  blocking collectives  86.6 us (20%)
  other arithmetic  63.8 us (15%)
  local copies, waits for them, and re-layouts  51.2 us (12%)
  matrix products  28.1 us (7%)
  between operations  13.4 us (3%)
    reduce_scatter x1, waiting for transfers between devices, per_device(): lax.psum_scatter(down_terms, 'seq', scatter_dimension=1, tiled=True)  69.2 us
    all_gather x2, blocking collectives, combined_all(): pieces = jax.tree.map(lambda part: lax.all_gather(part, axis), value)  62.8 us
    psum x1, waiting for transfers between devices, per_device(): local_x = lax.psum(partial_x.astype(jnp.bfloat16), ('tok', 'kv'))  61.3 us
    add x15, other arithmetic, combine(): accum_a * factor_a[..., None] + accum_b * factor_b[..., None]  38.7 us
    reduce_scatter x1, waiting for transfers between devices, per_device(): lax.psum_scatter(jnp.dot(slot_rows, proj_out, preferred_element_type=jnp....  28.3 us
    all_gather x1, blocking collectives, per_device(): lax.all_gather(mid, 'seq', axis=1, tiled=True).astype(jnp.float32)  23.9 us
    unnamed x25, local copies, waits for them, and re-layouts  22.3 us
    all_gather x1, waiting for transfers between devices, per_device(): full_x = lax.all_gather(local_x, 'seq', axis=1, tiled=True)  21.2 us
  transfers between devices with their start and end apart: 5, of which 5 were waited for; matrix products, arithmetic and copies ran while one was open for 9% of the time, Pallas kernels for 0%

commit v1 on v0

--- a/solution.py
+++ b/solution.py
@@ -6,6 +6,19 @@
 EPSILON = 1e-05
 ROPE_BASE = 1000000.0
 FLOOR_SCORE = -1e30
+
+
+def gather_around(x, axis, dim):
+    ways = lax.axis_size(axis)
+    up = [(d, (d + 1) % ways) for d in range(ways)]
+    down = [(d, (d - 1) % ways) for d in range(ways)]
+    earlier, later = ([x], [x])
+    for _ in range(ways // 2):
+        earlier.append(lax.ppermute(earlier[-1], axis, up))
+    for _ in range((ways - 1) // 2):
+        later.append(lax.ppermute(later[-1], axis, down))
+    line = jnp.concatenate([*earlier[::-1], *later[1:]], axis=dim)
+    return jnp.roll(line, (lax.axis_index(axis) - ways // 2) * x.shape[dim], axis=dim)
 
 
 def combined_all(value, axis, join):
@@ -146,7 +159,7 @@
         per_owner * n_steps, columns
     )
     mid = (own_x.astype(jnp.float32) + attn_part).astype(jnp.bfloat16)
-    piece_wide = lax.all_gather(mid, "seq", axis=1, tiled=True).astype(jnp.float32)
+    piece_wide = gather_around(mid, "seq", 1).astype(jnp.float32)
     gain_part = mlp_gain.astype(jnp.float32)
     piece_scaled = (piece_wide * gain_part).astype(jnp.bfloat16)
     gate_acc = jnp.dot(piece_scaled, proj_gate, preferred_element_type=jnp.float32)

time: 432 us -> 466 us (1.079)
  starting transfers between devices: 0.17 us -> 39.2 us
  blocking collectives: 86.6 us -> 61.8 us
  waiting for transfers between devices: 186 us -> 204 us
    ppermute x0 -> x15, starting transfers between devices: none -> 39 us  [the longest x7 37.5 us: gather_around(): later.append(lax.ppermute(later[-1], axis, down))]
    all_gather x1 -> x0, blocking collectives: 23.9 us -> none  [per_device(): lax.all_gather(mid, 'seq', axis=1, tiled=True).astype(jnp.float32)]
    ppermute x0 -> x15, waiting for transfers between devices: none -> 16.7 us  [the longest x8 16.7 us: gather_around(): earlier.append(lax.ppermute(earlier[-1], axis, up))]
    unnamed x25 -> x54, local copies, waits for them, and re-layouts: 22.3 us -> 22.9 us
  transfers between devices with their start and end apart: 5 -> 20, of which waited for: 5 -> 13; matrix products, arithmetic and copies ran while one was open for 9% -> 9% of each run, Pallas kernels for 0% -> 0%
where the time goes in v1:
time: 466 us; the launch traced here: 464 us
  waiting for transfers between devices  204 us (44%)
  other arithmetic  64.4 us (14%)
  blocking collectives  61.8 us (13%)
  local copies, waits for them, and re-layouts  51.7 us (11%)
  starting transfers between devices  39.2 us (8%)
  matrix products  28.1 us (6%)
  between operations  13.5 us (3%)
    reduce_scatter x1, waiting for transfers between devices, per_device(): lax.psum_scatter(down_terms, 'seq', scatter_dimension=1, tiled=True)  70.8 us
    all_gather x2, blocking collectives, combined_all(): pieces = jax.tree.map(lambda part: lax.all_gather(part, axis), value)  61.8 us
    psum x1, waiting for transfers between devices, per_device(): local_x = lax.psum(partial_x.astype(jnp.bfloat16), ('tok', 'kv'))  61.3 us
    add x15, other arithmetic, combine(): accum_a * factor_a[..., None] + accum_b * factor_b[..., None]  38.7 us
    ppermute x7, starting transfers between devices, gather_around(): later.append(lax.ppermute(later[-1], axis, down))  37.5 us
    reduce_scatter x1, waiting for transfers between devices, per_device(): lax.psum_scatter(jnp.dot(slot_rows, proj_out, preferred_element_type=jnp....  27.4 us
    unnamed x54, local copies, waits for them, and re-layouts  22.9 us
    all_gather x1, waiting for transfers between devices, per_device(): full_x = lax.all_gather(local_x, 'seq', axis=1, tiled=True)  20.9 us
  transfers between devices with their start and end apart: 20, of which 13 were waited for; matrix products, arithmetic and copies ran while one was open for 9% of the time, Pallas kernels for 0%

profile of v1, /device:TPU:0, one launch (start us, length us, event | category | flops | bytes accessed | tf_op | source)
XLA Modules:
  0.0 463.6 jit_solution(14796756354406097704)
XLA Ops:
  6.5 0.8 compare_and_fusion.1
  9.9 2.1 gather_fusion
  12.8 61.3 %all-reduce.2.cloned.1.call-done = bf16[256,128]{1,0:T(8,128)(2,1)} async-done(((bf16[256,128]{1,0:T(8,128)(2,1)}), bf16[256,128]{1,0:T(8,128)(2,1)}) %all-reduce.2.cloned.1.call-update) | async-done | bytes 65552 | tf_op jit(solution)/shard_map/psum | solution.py:89
  74.9 22.4 %copy.87 = bf16[64,1024,1,128]{1,3,0,2:T(8,128)(2,1)} copy(bf16[64,1024,1,128]{3,1,2,0:T(8,128)(2,1)} %param.22) | data formatting | bytes 33554432 | tf_op args[7]
  98.0 20.9 %all-gather.6.cloned.1.call-done = bf16[256,2048]{1,0:T(8,128)(2,1)} async-done(((bf16[256,128]{1,0:T(8,128)(2,1)}), bf16[256,2048]{1,0:T(8,128)(2,1)}) %all-gather.6.cloned.1.call-update) | async-done | bytes 1048592 | tf_op jit(solution)/shard_map/all_gather | solution.py:91
  118.9 1.5 fusion.7
  120.4 2.0 convolution_multiply_fusion.1
  122.7 1.8 convolution_multiply_fusion.2
  124.8 1.0 multiply_cosine_fusion
  126.5 6.2 %fusion.5 = (f32[64,4,4]{2,1,0:T(4,128)S(1)}, f32[64,4,4,1024]{3,2,1,0:T(4,128)S(1)}) fusion(pred[64,1024]{1,0:T(8,128)(4,1)} %broadcast_compare_fusion, bf16[64,1024,128]{1,2,0:T(8,128)(2,1)} %bitcast.67, bf16[64,4,4,32]{3,2,1,0:T(4,128)(2,1)S(1)} %get-tuple-element.101, bf16[64,4,4,32]{3,2,1,0:T(4,128)(2,1)S(1)} %get-tuple-element.100), kind=kOutput, calls=%fused_computation.18 | convolution fusion | flops 137624576 | bytes 12783616 | tf_op jit(solution)/shard_map/rjgd,rpd->rjgp/dot_general | solution.py:110
  132.6 3.7 convert_reduce_fusion
  136.4 6.8 %fusion.3 = f32[64,4,4,64]{3,2,1,0:T(4,128)} fusion(bf16[64,4,4,1024]{3,2,1,0:T(4,128)(2,1)S(1)} %get-tuple-element.99, bf16[64,1024,128]{1,2,0:T(8,128)(2,1)} %bitcast.68), kind=kOutput, calls=%fused_computation.12 | convolution fusion | flops 134217728 | bytes 10747904 | tf_op jit(solution)/shard_map/rjgp,rpd->rjgd/dot_general | solution.py:120
  143.3 30.5 %all-gather.1 = f32[1024,4,4]{2,1,0:T(4,128)S(1)} all-gather(f32[64,4,4]{2,1,0:T(4,128)S(1)} %get-tuple-element.98), channel_id=3, replica_groups=mesh['tok'=4,'seq'=16,'kv'=2] {'seq'}, dimensions={0}, use_global_device_ids=true | all-gather | bytes 69632 | tf_op jit(solution)/shard_map/all_gather | solution.py:25
  173.8 1.4 slice.76
  175.2 31.3 %all-gather = f32[1024,4,4]{2,1,0:T(4,128)S(1)} all-gather(f32[64,4,4]{2,1,0:T(4,128)S(1)} %get-tuple-element.110), channel_id=2, replica_groups=mesh['tok'=4,'seq'=16,'kv'=2] {'seq'}, dimensions={0}, use_global_device_ids=true | all-gather | bytes 69632 | tf_op jit(solution)/shard_map/all_gather | solution.py:25
  206.6 1.5 slice.75
  208.8 3.3 fusion.39
  213.3 1.0 copy.102
  214.4 2.6 copy.93
  217.1 2.2 copy.92
  219.2 7.1 %all-gather.8.cloned.1.call-done = f32[1024,4,4,64]{3,2,1,0:T(4,128)} async-done(((f32[64,4,4,64]{3,2,1,0:T(4,128)}), f32[1024,4,4,64]{3,2,1,0:T(4,128)}) %all-gather.8.cloned.1.call-update) | async-done | bytes 4194320 | tf_op jit(solution)/shard_map/all_gather | solution.py:25
  226.4 7.7 %slice.77 = f32[960,4,4,64]{3,2,1,0:T(4,128)} slice(f32[1024,4,4,64]{3,2,1,0:T(4,128)} %all-gather.8.cloned.1.call-done), slice={[64:1024], [0:4], [0:4], [0:64]} | slice | bytes 7864320 | tf_op jit(solution)/shard_map/slice | solution.py:27
  234.1 53.9 %while.14 = (s32[]{:T(128)}, f32[64,4,4]{0,2,1:T(4,128)S(1)}, f32[64,4,4]{0,2,1:T(4,128)S(1)}, f32[64,4,4,64]{3,2,1,0:T(4,128)S(1)}, f32[15,64,4,4]{1,3,2,0:T(4,...) while((s32[]{:T(128)}, f32[64,4,4]{0,2,1:T(4,128)S(1)}, ...), condition=%wide.region_5.6_spmd, body=%wide.region_4.5_spmd.sunk | while | flops 202754 | bytes 843877 | solution.py:28
  235.1 2.6 fusion.57
  238.7 2.6 fusion.57
  242.3 2.6 fusion.57
  245.9 2.6 fusion.57
  249.5 2.6 fusion.57
  253.1 2.6 fusion.57
  256.7 2.6 fusion.57
  260.3 2.6 fusion.57
  263.9 2.6 fusion.57
  267.4 2.6 fusion.57
  271.0 2.6 fusion.57
  274.6 2.6 fusion.57
  278.2 2.6 fusion.57
  281.8 2.6 fusion.57
  285.4 2.6 fusion.57
  288.2 0.8 copy.104
  289.7 2.0 fusion.10
  291.9 0.8 gather_fusion.2
  292.8 0.8 fusion.44
  293.8 1.4 gather_fusion.1
  295.2 27.4 %reduce-scatter.3.cloned.1.call-done = f32[32,128]{1,0:T(8,128)} async-done(((f32[256,128]{1,0:T(8,128)}), f32[32,128]{1,0:T(8,128)}) %reduce-scatter.3.cloned.1.call-update) | async-done | bytes 16400 | tf_op jit(solution)/shard_map/reduce_scatter | solution.py:151
  323.3 1.5 collective-permute-start
  324.9 5.5 %collective-permute-done = bf16[32,128]{1,0:T(8,128)(2,1)S(1)} collective-permute-done((bf16[32,128]{1,0:T(8,128)(2,1)S(1)}, bf16[32,128]{1,0:T(8,128)(2,1)S(1)}, u32[]{:S(2)}, u32[]{:S(2)}) %collective-permute-start) | collective-permute-done | bytes 8224 | tf_op jit(solution)/shard_map/ppermute | solution.py:17
  330.3 5.3 %collective-permute-start.8 = (bf16[32,128]{1,0:T(8,128)(2,1)S(1)}, bf16[32,128]{1,0:T(8,128)(2,1)S(1)}, u32[]{:S(2)}, u32[]{:S(2)}) collective-permute-start(bf16[32,128]{1,0:T(8,128)(2,1)S(1)} %fusion.32), channel_id=1, source_target_pairs={{0,30},{2,0},{4,2},{6,4},{8,6},{10,8},{12,10},{14,12},{16,14},{18,... | collective-permute-start | bytes 24584 | tf_op jit(solution)/shard_map/ppermute | solution.py:19
  335.7 1.6 collective-permute-done.1
  337.3 5.3 %collective-permute-start.9 = (bf16[32,128]{1,0:T(8,128)(2,1)S(1)}, bf16[32,128]{1,0:T(8,128)(2,1)S(1)}, u32[]{:S(2)}, u32[]{:S(2)}) collective-permute-start(bf16[32,128]{1,0:T(8,128)(2,1)S(1)} %collective-permute-done.8), channel_id=1, source_target_pairs={{0,30},{2,0},{4,2},{6,4},{8,6},{10,8},{12,10},{14,12},{16,14},{18,... | collective-permute-start | bytes 24584 | tf_op jit(solution)/shard_map/ppermute | solution.py:19
  342.6 1.6 collective-permute-done.2
  344.3 5.3 %collective-permute-start.10 = (bf16[32,128]{1,0:T(8,128)(2,1)S(1)}, bf16[32,128]{1,0:T(8,128)(2,1)S(1)}, u32[]{:S(2)}, u32[]{:S(2)}) collective-permute-start(bf16[32,128]{1,0:T(8,128)(2,1)S(1)} %collective-permute-done.9), channel_id=1, source_target_pairs={{0,30},{2,0},{4,2},{6,4},{8,6},{10,8},{12,10},{14,12},{16,14},{18,... | collective-permute-start | bytes 24584 | tf_op jit(solution)/shard_map/ppermute | solution.py:19
  349.6 1.6 collective-permute-done.3
  351.2 5.3 %collective-permute-start.11 = (bf16[32,128]{1,0:T(8,128)(2,1)S(1)}, bf16[32,128]{1,0:T(8,128)(2,1)S(1)}, u32[]{:S(2)}, u32[]{:S(2)}) collective-permute-start(bf16[32,128]{1,0:T(8,128)(2,1)S(1)} %collective-permute-done.10), channel_id=1, source_target_pairs={{0,30},{2,0},{4,2},{6,4},{8,6},{10,8},{12,10},{14,12},{16,14},{18,... | collective-permute-start | bytes 24584 | tf_op jit(solution)/shard_map/ppermute | solution.py:19
  356.6 1.6 collective-permute-done.4
  358.2 5.3 %collective-permute-start.12 = (bf16[32,128]{1,0:T(8,128)(2,1)S(1)}, bf16[32,128]{1,0:T(8,128)(2,1)S(1)}, u32[]{:S(2)}, u32[]{:S(2)}) collective-permute-start(bf16[32,128]{1,0:T(8,128)(2,1)S(1)} %collective-permute-done.11), channel_id=1, source_target_pairs={{0,30},{2,0},{4,2},{6,4},{8,6},{10,8},{12,10},{14,12},{16,14},{18,... | collective-permute-start | bytes 24584 | tf_op jit(solution)/shard_map/ppermute | solution.py:19
  363.5 1.6 collective-permute-done.5
  365.2 5.3 %collective-permute-start.13 = (bf16[32,128]{1,0:T(8,128)(2,1)S(1)}, bf16[32,128]{1,0:T(8,128)(2,1)S(1)}, u32[]{:S(2)}, u32[]{:S(2)}) collective-permute-start(bf16[32,128]{1,0:T(8,128)(2,1)S(1)} %collective-permute-done.12), channel_id=1, source_target_pairs={{0,30},{2,0},{4,2},{6,4},{8,6},{10,8},{12,10},{14,12},{16,14},{18,... | collective-permute-start | bytes 24584 | tf_op jit(solution)/shard_map/ppermute | solution.py:19
  370.5 1.6 collective-permute-done.6
  372.2 5.4 %collective-permute-start.14 = (bf16[32,128]{1,0:T(8,128)(2,1)S(1)}, bf16[32,128]{1,0:T(8,128)(2,1)S(1)}, u32[]{:S(2)}, u32[]{:S(2)}) collective-permute-start(bf16[32,128]{1,0:T(8,128)(2,1)S(1)} %collective-permute-done.13), channel_id=1, source_target_pairs={{0,30},{2,0},{4,2},{6,4},{8,6},{10,8},{12,10},{14,12},{16,14},{18,... | collective-permute-start | bytes 24584 | tf_op jit(solution)/shard_map/ppermute | solution.py:19
  377.6 1.5 collective-permute-done.7
  379.7 2.0 convolution_multiply_fusion.4
  381.7 3.2 fusion.13
  384.9 70.8 %reduce-scatter.5.cloned.1.call-done = f32[32,128]{1,0:T(8,128)} async-done(((f32[32,2048]{1,0:T(8,128)}), f32[32,128]{1,0:T(8,128)}) %reduce-scatter.5.cloned.1.call-update) | async-done | bytes 16400 | tf_op jit(solution)/shard_map/reduce_scatter | solution.py:171
  455.7 1.3 add_convert_fusion.2
  (168 shorter events, 25.6 us)
Async XLA Ops:
  6.5 375.2 %copy-start = (bf16[512,2048]{1,0:T(8,128)(2,1)S(1)}, bf16[512,2048]{1,0:T(8,128)(2,1)}, u32[]{:S(2)}) copy-start(bf16[512,2048]{1,0:T(8,128)(2,1)} %param.27) | copy-start | bytes 6291460
  6.5 67.6 %all-reduce.2.cloned.1.call-start = ((), (), s32[]{:S(2)}) async-start(), calls=%async_computation.2 | async-start | bytes 131072 | tf_op jit(solution)/shard_map/psum | solution.py:89
  12.8 106.1 %all-gather.6.cloned.1.call-start = ((), (), s32[]{:S(2)}) async-start(), calls=%async_computation.3 | async-start | bytes 1114112 | tf_op jit(solution)/shard_map/all_gather | solution.py:91
  74.1 152.2 %all-gather.8.cloned.1.call-start = ((), (), s32[]{:S(2)}) async-start(), calls=%async_computation.6 | async-start | bytes 8912896 | tf_op jit(solution)/shard_map/all_gather | solution.py:25
  74.9 22.4 %copy-start.7 = (s32[64]{0:T(128)S(1)}, s32[64]{0:T(128)}, u32[]{:S(2)}) copy-start(s32[64]{0:T(128)} %param.17) | copy-start | bytes 772
  126.5 6.2 %copy-start.1 = (pred[64,1024]{1,0:T(8,128)(4,1)S(1)}, pred[64,1024]{1,0:T(8,128)(4,1)}, u32[]{:S(2)}) copy-start(pred[64,1024]{1,0:T(8,128)(4,1)} %broadcast_compare_fusion) | copy-start | bytes 196612
  143.2 179.4 %reduce-scatter.3.cloned.1.call-start = ((), (), s32[]{:S(2)}) async-start(), calls=%async_computation.4 | async-start | bytes 147456 | tf_op jit(solution)/shard_map/reduce_scatter | solution.py:151
  143.3 69.2 %copy-start.8 = (pred[4,4]{1,0:T(4,128)(4,1)}, pred[4,4]{1,0:T(4,128)(4,1)S(1)}, u32[]{:S(2)}) copy-start(pred[4,4]{1,0:T(4,128)(4,1)S(1)} %iota_compare_fusion) | copy-start | bytes 52
  175.2 32.8 %copy-start.3 = (bf16[64,4,32]{0,2,1:T(8,128)(2,1)S(1)}, bf16[64,4,32]{0,2,1:T(8,128)(2,1)}, u32[]{:S(2)}) copy-start(bf16[64,4,32]{0,2,1:T(8,128)(2,1)} %get-tuple-element.108) | copy-start | bytes 49156
  175.2 32.8 %copy-start.4 = (bf16[64,4,32]{0,2,1:T(8,128)(2,1)S(1)}, bf16[64,4,32]{0,2,1:T(8,128)(2,1)}, u32[]{:S(2)}) copy-start(bf16[64,4,32]{0,2,1:T(8,128)(2,1)} %get-tuple-element.109) | copy-start | bytes 49156
  226.4 7.7 %slice-start = ((f32[1024,4,4,64]{3,2,1,0:T(4,128)}), f32[64,4,4,64]{3,2,1,0:T(4,128)S(1)}, s32[]{:S(2)}) async-start(f32[1024,4,4,64]{3,2,1,0:T(4,128)} %all-gather.8.cloned.1.call-done), calls=%async_computation.7 | async-start | bytes 1048576 | tf_op jit(solution)/shard_map/slice | solution.py:26
  234.1 55.6 %copy-start.2 = (bf16[64,4,4,4]{3,2,1,0:T(4,128)(2,1)S(1)}, bf16[64,4,4,4]{3,2,1,0:T(4,128)(2,1)}, u32[]{:S(2)}) copy-start(bf16[64,4,4,4]{3,2,1,0:T(4,128)(2,1)} %copy.102) | copy-start | bytes 24580
  289.7 3.1 copy-start.5
  289.7 4.0 copy-start.9
  289.7 82.4 %copy-start.6 = (bf16[2048]{0:T(1024)(128)(2,1)S(1)}, bf16[2048]{0:T(1024)(128)(2,1)}, u32[]{:S(2)}) copy-start(bf16[2048]{0:T(1024)(128)(2,1)} %param.24) | copy-start | bytes 12292
  293.6 162.1 %reduce-scatter.5.cloned.1.call-start = ((), (), s32[]{:S(2)}) async-start(), calls=%async_computation.5 | async-start | bytes 278528 | tf_op jit(solution)/shard_map/reduce_scatter | solution.py:171
  323.3 7.0 %collective-permute-start = (bf16[32,128]{1,0:T(8,128)(2,1)S(1)}, bf16[32,128]{1,0:T(8,128)(2,1)S(1)}, u32[]{:S(2)}, u32[]{:S(2)}) collective-permute-start(bf16[32,128]{1,0:T(8,128)(2,1)S(1)} %fusion.32), channel_id=1, source_target_pairs={{0,2},{2,4},{4,6},{6,8},{8,10},{10,12},{12,14},{14,16},{16,18},{18... | collective-permute-start | bytes 24584 | tf_op jit(solution)/shard_map/ppermute | solution.py:17
  330.3 7.0 %collective-permute-start.1 = (bf16[32,128]{1,0:T(8,128)(2,1)S(1)}, bf16[32,128]{1,0:T(8,128)(2,1)S(1)}, u32[]{:S(2)}, u32[]{:S(2)}) collective-permute-start(bf16[32,128]{1,0:T(8,128)(2,1)S(1)} %collective-permute-done), channel_id=1, source_target_pairs={{0,2},{2,4},{4,6},{6,8},{8,10},{10,12},{12,14},{14,16},{16,18},{18... | collective-permute-start | bytes 24584 | tf_op jit(solution)/shard_map/ppermute | solution.py:17
  330.3 7.0 %collective-permute-start.8 = (bf16[32,128]{1,0:T(8,128)(2,1)S(1)}, bf16[32,128]{1,0:T(8,128)(2,1)S(1)}, u32[]{:S(2)}, u32[]{:S(2)}) collective-permute-start(bf16[32,128]{1,0:T(8,128)(2,1)S(1)} %fusion.32), channel_id=1, source_target_pairs={{0,30},{2,0},{4,2},{6,4},{8,6},{10,8},{12,10},{14,12},{16,14},{18,... | collective-permute-start | bytes 24584 | tf_op jit(solution)/shard_map/ppermute | solution.py:19
  337.3 7.0 %collective-permute-start.2 = (bf16[32,128]{1,0:T(8,128)(2,1)S(1)}, bf16[32,128]{1,0:T(8,128)(2,1)S(1)}, u32[]{:S(2)}, u32[]{:S(2)}) collective-permute-start(bf16[32,128]{1,0:T(8,128)(2,1)S(1)} %collective-permute-done.1), channel_id=1, source_target_pairs={{0,2},{2,4},{4,6},{6,8},{8,10},{10,12},{12,14},{14,16},{16,18},{18... | collective-permute-start | bytes 24584 | tf_op jit(solution)/shard_map/ppermute | solution.py:17
  337.3 7.0 %collective-permute-start.9 = (bf16[32,128]{1,0:T(8,128)(2,1)S(1)}, bf16[32,128]{1,0:T(8,128)(2,1)S(1)}, u32[]{:S(2)}, u32[]{:S(2)}) collective-permute-start(bf16[32,128]{1,0:T(8,128)(2,1)S(1)} %collective-permute-done.8), channel_id=1, source_target_pairs={{0,30},{2,0},{4,2},{6,4},{8,6},{10,8},{12,10},{14,12},{16,14},{18,... | collective-permute-start | bytes 24584 | tf_op jit(solution)/shard_map/ppermute | solution.py:19
  344.3 7.0 %collective-permute-start.3 = (bf16[32,128]{1,0:T(8,128)(2,1)S(1)}, bf16[32,128]{1,0:T(8,128)(2,1)S(1)}, u32[]{:S(2)}, u32[]{:S(2)}) collective-permute-start(bf16[32,128]{1,0:T(8,128)(2,1)S(1)} %collective-permute-done.2), channel_id=1, source_target_pairs={{0,2},{2,4},{4,6},{6,8},{8,10},{10,12},{12,14},{14,16},{16,18},{18... | collective-permute-start | bytes 24584 | tf_op jit(solution)/shard_map/ppermute | solution.py:17
  344.3 7.0 %collective-permute-start.10 = (bf16[32,128]{1,0:T(8,128)(2,1)S(1)}, bf16[32,128]{1,0:T(8,128)(2,1)S(1)}, u32[]{:S(2)}, u32[]{:S(2)}) collective-permute-start(bf16[32,128]{1,0:T(8,128)(2,1)S(1)} %collective-permute-done.9), channel_id=1, source_target_pairs={{0,30},{2,0},{4,2},{6,4},{8,6},{10,8},{12,10},{14,12},{16,14},{18,... | collective-permute-start | bytes 24584 | tf_op jit(solution)/shard_map/ppermute | solution.py:19
  351.2 7.0 %collective-permute-start.4 = (bf16[32,128]{1,0:T(8,128)(2,1)S(1)}, bf16[32,128]{1,0:T(8,128)(2,1)S(1)}, u32[]{:S(2)}, u32[]{:S(2)}) collective-permute-start(bf16[32,128]{1,0:T(8,128)(2,1)S(1)} %collective-permute-done.3), channel_id=1, source_target_pairs={{0,2},{2,4},{4,6},{6,8},{8,10},{10,12},{12,14},{14,16},{16,18},{18... | collective-permute-start | bytes 24584 | tf_op jit(solution)/shard_map/ppermute | solution.py:17
  351.2 7.0 %collective-permute-start.11 = (bf16[32,128]{1,0:T(8,128)(2,1)S(1)}, bf16[32,128]{1,0:T(8,128)(2,1)S(1)}, u32[]{:S(2)}, u32[]{:S(2)}) collective-permute-start(bf16[32,128]{1,0:T(8,128)(2,1)S(1)} %collective-permute-done.10), channel_id=1, source_target_pairs={{0,30},{2,0},{4,2},{6,4},{8,6},{10,8},{12,10},{14,12},{16,14},{18,... | collective-permute-start | bytes 24584 | tf_op jit(solution)/shard_map/ppermute | solution.py:19
  358.2 7.0 %collective-permute-start.5 = (bf16[32,128]{1,0:T(8,128)(2,1)S(1)}, bf16[32,128]{1,0:T(8,128)(2,1)S(1)}, u32[]{:S(2)}, u32[]{:S(2)}) collective-permute-start(bf16[32,128]{1,0:T(8,128)(2,1)S(1)} %collective-permute-done.4), channel_id=1, source_target_pairs={{0,2},{2,4},{4,6},{6,8},{8,10},{10,12},{12,14},{14,16},{16,18},{18... | collective-permute-start | bytes 24584 | tf_op jit(solution)/shard_map/ppermute | solution.py:17
  358.2 7.0 %collective-permute-start.12 = (bf16[32,128]{1,0:T(8,128)(2,1)S(1)}, bf16[32,128]{1,0:T(8,128)(2,1)S(1)}, u32[]{:S(2)}, u32[]{:S(2)}) collective-permute-start(bf16[32,128]{1,0:T(8,128)(2,1)S(1)} %collective-permute-done.11), channel_id=1, source_target_pairs={{0,30},{2,0},{4,2},{6,4},{8,6},{10,8},{12,10},{14,12},{16,14},{18,... | collective-permute-start | bytes 24584 | tf_op jit(solution)/shard_map/ppermute | solution.py:19
  365.2 7.0 %collective-permute-start.6 = (bf16[32,128]{1,0:T(8,128)(2,1)S(1)}, bf16[32,128]{1,0:T(8,128)(2,1)S(1)}, u32[]{:S(2)}, u32[]{:S(2)}) collective-permute-start(bf16[32,128]{1,0:T(8,128)(2,1)S(1)} %collective-permute-done.5), channel_id=1, source_target_pairs={{0,2},{2,4},{4,6},{6,8},{8,10},{10,12},{12,14},{14,16},{16,18},{18... | collective-permute-start | bytes 24584 | tf_op jit(solution)/shard_map/ppermute | solution.py:17
  365.2 7.0 %collective-permute-start.13 = (bf16[32,128]{1,0:T(8,128)(2,1)S(1)}, bf16[32,128]{1,0:T(8,128)(2,1)S(1)}, u32[]{:S(2)}, u32[]{:S(2)}) collective-permute-start(bf16[32,128]{1,0:T(8,128)(2,1)S(1)} %collective-permute-done.12), channel_id=1, source_target_pairs={{0,30},{2,0},{4,2},{6,4},{8,6},{10,8},{12,10},{14,12},{16,14},{18,... | collective-permute-start | bytes 24584 | tf_op jit(solution)/shard_map/ppermute | solution.py:19
  372.1 7.0 %collective-permute-start.7 = (bf16[32,128]{1,0:T(8,128)(2,1)S(1)}, bf16[32,128]{1,0:T(8,128)(2,1)S(1)}, u32[]{:S(2)}, u32[]{:S(2)}) collective-permute-start(bf16[32,128]{1,0:T(8,128)(2,1)S(1)} %collective-permute-done.6), channel_id=1, source_target_pairs={{0,2},{2,4},{4,6},{6,8},{8,10},{10,12},{12,14},{14,16},{16,18},{18... | collective-permute-start | bytes 24584 | tf_op jit(solution)/shard_map/ppermute | solution.py:17
  372.2 7.1 %collective-permute-start.14 = (bf16[32,128]{1,0:T(8,128)(2,1)S(1)}, bf16[32,128]{1,0:T(8,128)(2,1)S(1)}, u32[]{:S(2)}, u32[]{:S(2)}) collective-permute-start(bf16[32,128]{1,0:T(8,128)(2,1)S(1)} %collective-permute-done.13), channel_id=1, source_target_pairs={{0,30},{2,0},{4,2},{6,4},{8,6},{10,8},{12,10},{14,12},{16,14},{18,... | collective-permute-start | bytes 24584 | tf_op jit(solution)/shard_map/ppermute | solution.py:19
Sparse Core Ops, SparseCore 0:
  12.9 61.1 all-reduce.1
  76.4 42.4 all-gather.5
  143.4 82.9 all-gather.7
  293.7 28.8 reduce-scatter.2
  385.1 70.6 reduce-scatter.4
